TPU v7x, 128 devices: a whole 4x4x4 slice. The times are simulated.
128 devices in a mesh: pos: 16 (over x, y), obj: 8 (over z, core).
Axes of the slice: x: 4, y: 4, z: 4, core: 2. Of those that a mesh axis runs over, the one named last changes fastest.
Arguments:
- object_field: float32 [2, 4096, 6144], P(None, 'obj', 'pos'), may hold values from -5 to 5
- probe: float32 [2, 256, 256], replicated, may hold values from -5 to 5
- amplitude: bfloat16 [2048, 256, 256], P(('pos', 'obj')), may hold values from 0.19921875 to 3
- row_offset: int32 [2048], P(('pos', 'obj')), may hold values from 0 to 256
- col_offset: int32 [2048], P(('pos', 'obj')), may hold values from 0 to 128
- owner: int32 [2048], P(('pos', 'obj')), may hold values from 0 to 15, as said below
Outputs:
- new_object: float32 [2, 4096, 6144], P(None, 'obj', 'pos')
- new_probe: float32 [2, 256, 256], replicated
Inputs may be any that keep to these rules, and one draw needn't show every extreme that they name: Among the 16 positions of one device no owner is named more than 2 times; in each row band one owner is named exactly 2 times by every device.
All inputs are finite; a program needn't handle non-finite values.
Results may differ from a plain program's by a relative error of at most 0.005.
The roundings to bfloat16 on the way count: a program that leaves them out, or rounds other values in their place, can miss the bound.
Values may be sent and summed in bfloat16 or wider, within the bound.
A program may use at most 128 MiB of HBM per device.

v0:
```python
import math
import jax
import jax.numpy as jnp
from jax import lax
from jax.sharding import PartitionSpec as P


def padded_2(block, sides, width):
    for axis, dim in sides:
        count = lax.axis_size(axis)
        forward = [(i, i + 1) for i in range(count - 1)]
        forward.append((count - 1, 0))
        backward = [(target, source) for source, target in forward]
        low = lax.ppermute(
            lax.slice_in_dim(block, block.shape[dim] - width, None, axis=dim), axis, forward
        )
        high = lax.ppermute(lax.slice_in_dim(block, 0, width, axis=dim), axis, backward)
        block = jnp.concatenate([low, block, high], axis=dim)
    return block


def dft_tables(size):
    index = jnp.arange(size, dtype=jnp.int32)
    product = index[:, None] * index[None, :] % size
    angle = product.astype(jnp.float32) * (2.0 * math.pi / size)
    scale = 1.0 / math.sqrt(size)
    real_part = (jnp.cos(angle) * scale).astype(jnp.bfloat16)
    imag_part = (-jnp.sin(angle) * scale).astype(jnp.bfloat16)
    return (real_part, imag_part)


def left_apply(mat_re, mat_im, val_re, val_im):

    def product(matrix, values):
        return jnp.einsum("jk,bkl->bjl", matrix, values, preferred_element_type=jnp.float32)

    return (
        product(mat_re, val_re) - product(mat_im, val_im),
        product(mat_re, val_im) + product(mat_im, val_re),
    )


def right_apply(val_re, val_im, mat_re, mat_im):

    def product(values, matrix):
        return jnp.einsum("bjk,kl->bjl", values, matrix, preferred_element_type=jnp.float32)

    return (
        product(val_re, mat_re) - product(val_im, mat_im),
        product(val_re, mat_im) + product(val_im, mat_re),
    )


def position_terms(patches, amps, validity, probe, tables):
    four_re, four_im, conj_im = tables
    patch_re = patches[:, 0].astype(jnp.float32)
    patch_im = patches[:, 1].astype(jnp.float32)
    probe_re = probe[0]
    probe_im = probe[1]
    psi_re = (probe_re * patch_re - probe_im * patch_im).astype(jnp.bfloat16)
    psi_im = (probe_re * patch_im + probe_im * patch_re).astype(jnp.bfloat16)
    left_re, left_im = left_apply(four_re, four_im, psi_re, psi_im)
    wave_re, wave_im = right_apply(
        left_re.astype(jnp.bfloat16), left_im.astype(jnp.bfloat16), four_re, four_im
    )
    magnitude = jnp.sqrt(wave_re * wave_re + wave_im * wave_im)
    factor = 1.0 - amps.astype(jnp.float32) / jnp.maximum(magnitude, 0.5)
    diff_re = (wave_re * factor).astype(jnp.bfloat16)
    diff_im = (wave_im * factor).astype(jnp.bfloat16)
    back_re, back_im = left_apply(four_re, conj_im, diff_re, diff_im)
    chi_re, chi_im = right_apply(
        back_re.astype(jnp.bfloat16), back_im.astype(jnp.bfloat16), four_re, conj_im
    )
    chi_re = chi_re * validity[:, None, None]
    chi_im = chi_im * validity[:, None, None]
    grad_re = (probe_re * chi_re + probe_im * chi_im).astype(jnp.bfloat16)
    grad_im = (probe_re * chi_im - probe_im * chi_re).astype(jnp.bfloat16)
    term_re = jnp.sum(patch_re * chi_re + patch_im * chi_im, axis=0)
    term_im = jnp.sum(patch_re * chi_im - patch_im * chi_re, axis=0)
    return (jnp.stack([grad_re, grad_im], axis=1), jnp.stack([term_re, term_im]))


def run_terms(patches, amps, validity, probe, tables):
    count = patches.shape[0]
    size = patches.shape[2]
    batch_size = math.gcd(count, 8)
    groups = count // batch_size
    grouped = (
        patches.reshape(groups, batch_size, 2, size, size),
        amps.reshape(groups, batch_size, size, size),
        validity.reshape(groups, batch_size),
    )
    grads, terms = lax.map(
        lambda items: position_terms(items[0], items[1], items[2], probe, tables), grouped
    )
    return (grads.reshape(count, 2, size, size), jnp.sum(terms, axis=0))


def extract(tile, corners, size):
    zero = jnp.zeros((), jnp.int32)
    windows = jax.vmap(lambda row, col: lax.dynamic_slice(tile, (zero, row, col), (2, size, size)))(
        corners[:, 0], corners[:, 1]
    )
    return windows.astype(jnp.bfloat16)


def add_scaled(start_value, grads, corners, size):
    zero = jnp.zeros((), jnp.int32)

    def add_one(item, acc):
        corner = (zero, corners[item, 0], corners[item, 1])
        window = lax.dynamic_slice(acc, corner, (2, size, size))
        return lax.dynamic_update_slice(
            acc, window - 0.25 * grads[item].astype(jnp.float32), corner
        )

    return lax.fori_loop(0, grads.shape[0], add_one, start_value)


def shards(object_field, probe, amplitude, row_offset, col_offset, owner):
    n_pos = lax.axis_size("pos")
    n_obj = lax.axis_size("obj")
    pos_dev = amplitude.shape[0]
    size = amplitude.shape[1]
    capacity = max(2, pos_dev // n_pos + 1)
    slots = n_pos * capacity
    padded = padded_2(object_field.astype(jnp.bfloat16), (("pos", 2), ("obj", 1)), 1).astype(
        object_field.dtype
    )
    smooth = 4.0 * object_field - padded[:, :-2, 1:-1] - padded[:, 2:, 1:-1]
    smooth = smooth - padded[:, 1:-1, :-2] - padded[:, 1:-1, 2:]
    four_re, four_im = dft_tables(size)
    tables = (four_re, four_im, -four_im)
    onehot = (owner[:, None] == jnp.arange(n_pos, dtype=jnp.int32)[None, :]).astype(jnp.int32)
    earlier = jnp.cumsum(onehot, axis=0) - onehot
    ranking = jnp.sum(earlier * onehot, axis=1)
    target = owner * capacity + ranking
    matching = (target[:, None] == jnp.arange(slots, dtype=jnp.int32)[None, :]).astype(jnp.int32)
    source = jnp.sum(matching * jnp.arange(pos_dev, dtype=jnp.int32)[:, None], axis=0)
    filled = jnp.sum(matching, axis=0) > 0
    listing = jnp.stack([row_offset, col_offset, jnp.ones_like(row_offset)], axis=1)
    slot_info = jnp.where(filled[:, None], listing[source], 0).reshape(n_pos, capacity, 3)
    received = lax.all_to_all(slot_info, "pos", split_axis=0, concat_axis=0, tiled=True)
    items = received.shape[1]
    windows = extract(object_field, received.reshape(-1, 3), size)
    windows = windows.reshape(n_pos, items, 2, size, size)
    fetched = lax.all_to_all(windows, "pos", split_axis=0, concat_axis=0, tiled=True)
    mine = fetched.reshape(slots, 2, size, size)[target]
    grads, probe_part = run_terms(mine, amplitude, jnp.ones((pos_dev,), jnp.float32), probe, tables)
    grad_slots = jnp.where(filled[:, None, None, None], grads[source], jnp.zeros((), jnp.bfloat16))
    incoming = lax.all_to_all(
        grad_slots.reshape(n_pos, capacity, 2, size, size),
        "pos",
        split_axis=0,
        concat_axis=0,
        tiled=True,
    )
    incoming = incoming.reshape(slots, 2, size, size)
    corners = received.reshape(slots, 3)
    base = object_field - 0.125 * smooth
    new_object = add_scaled(base, incoming, corners, size)
    probe_grad = lax.psum(probe_part, ("pos", "obj"))
    n_total = pos_dev * n_pos * n_obj
    new_probe = probe - probe_grad * (1.0 / math.sqrt(n_total))
    return (new_object, new_probe)


def solution(mesh):
    placed = (
        P(None, "obj", "pos"),
        P(),
        P(("pos", "obj"), None, None),
        P(("pos", "obj")),
        P(("pos", "obj")),
        P(("pos", "obj")),
    )
    return jax.shard_map(
        shards, mesh=mesh, in_specs=placed, out_specs=(P(None, "obj", "pos"), P()), check_vma=False
    )
```

profile of v0, /device:TPU:15, one launch (start us, length us, event | category | flops | bytes accessed | tf_op | source)
XLA Modules:
  0.0 1008.5 jit_solution(17226852778361089383)
XLA Ops:
  12.1 6.8 all-to-all-start
  22.9 89.1 %while.29 = (s32[]{:T(128)}, bf16[2,512,384]{2,1,0:T(8,128)(2,1)S(1)}, s32[32,3]{0,1:T(4,128)S(1)}, bf16[32,2,256,256]{3,2,1,0:T(8,128)(2,1)}, s32[]{:T(128)}) while((s32[]{:T(128)}, bf16[2,512,384]{2,1,0:T(8,128)(2,1)S(1)}, s32[32,3]{0,1:T(4,128)S(1)}, bf16[32,2,256,256]{3,2,1,0:T(8,128)(2,1)}, s32[]{:T(128)}) %tuple.89), condition=%wide.while_cond, body=%wide.while_body.sunk | while | flops 2 | bytes 525929 | solution.py:101
  112.9 7.2 all-to-all-start.1
  120.1 130.6 %all-to-all-done.1 = bf16[16,2,2,256,256]{4,3,2,1,0:T(8,128)(2,1)} async-done(((bf16[16,2,2,256,256]{4,3,2,1,0:T(8,128)(2,1)}), bf16[16,2,2,256,256]{4,3,2,1,0:T(8,128)(2,1)}, u32[]{:S(2)}, u32[]{:S(2)}) %all-to-all-start.1) | async-done | bytes 8388640 | tf_op jit(solution)/shard_map/all_to_all | solution.py:147
  250.7 6.2 gather_fusion.1
  256.9 60.2 %while.30 = (s32[]{:T(128)}, bf16[2,8,2,256,256]{4,3,2,1,0:T(8,128)(2,1)}, f32[2,2,256,256]{3,2,1,0:T(8,128)S(1)}, f32[2,256,256]{2,1,0:T(8,128)S(1)}, bf16[2,8,...) while((s32[]{:T(128)}, ...), condition=%wide.region_7.8_spmd.clone.clone, body=%wide.region_4.7_spmd.clone.clone.sunk | while | flops 4348182528 | bytes 96470128 | solution.py:93
  282.5 3.0 fusion.253
  312.5 3.0 fusion.253
  317.1 7.5 gather_fusion.2
  324.6 7.2 broadcast_select_fusion
  331.8 9.4 all-to-all-start.2
  342.9 91.4 %collective-permute-done = bf16[2,512,1]{2,1,0:T(8,128)(2,1)S(1)} collective-permute-done((bf16[2,512,1]{2,1,0:T(8,128)(2,1)S(1)}, bf16[2,512,1]{2,1,0:T(8,128)(2,1)S(1)}, u32[]{:S(2)}, u32[]{:S(2)}) %collective-permute-start) | collective-permute-done | bytes 2080 | tf_op jit(solution)/shard_map/ppermute | solution.py:14
  435.7 11.3 %collective-permute-start.2 = (bf16[2,1,386]{2,1,0:T(2,128)(2,1)S(1)}, bf16[2,1,386]{2,1,0:T(2,128)(2,1)S(1)}, u32[]{:S(2)}, u32[]{:S(2)}) collective-permute-start(bf16[2,1,386]{2,1,0:T(2,128)(2,1)S(1)} %get-tuple-element.299), channel_id=1, source_target_pairs={{0,1},{1,2},{2,3},{3,4},{4,5},{5,6},{6,7},{7,0},{8,9},{9,10},{10,1... | collective-permute-start | bytes 4640 | tf_op jit(solution)/shard_map/ppermute | solution.py:14
  454.1 3.9 fusion.143
  458.0 151.4 %all-reduce.2.cloned.1.call-done = f32[2,256,256]{2,1,0:T(8,128)} async-done(((f32[2,256,256]{2,1,0:T(8,128)}), f32[2,256,256]{2,1,0:T(8,128)}) %all-reduce.2.cloned.1.call-update) | async-done | bytes 524304 | tf_op jit(solution)/shard_map/psum | solution.py:162
  611.3 390.4 %while.28 = (s32[]{:T(128)}, f32[2,512,384]{2,1,0:T(8,128)}, s32[32,3]{0,1:T(4,128)S(1)}, bf16[32,2,256,256]{3,2,1,0:T(8,128)(2,1)}, s32[]{:T(128)}, /*index=5*/s32[]{:T(128)}, s32[]{:T(128)}, s32[]{:T(128)}) while((s32[]{:T(128)}, f32[2,512,384]{2,1,0:T(8,128)}, s32[32,3]{0,1:T(4,128)S(1)}, bf16[32,2,256,256]{3,2,1,0:T(8,128)(2,1)}, ...), condition=%wide.region_9.10_spmd, body=%wide.region_8.9_spmd.sunk | while | flops 393224 | bytes 2359485 | solution.py:117
  617.2 6.4 dynamic_update_slice.24
  629.4 6.1 dynamic_update_slice.24
  641.4 6.5 dynamic_update_slice.24
  653.7 6.0 dynamic_update_slice.24
  665.7 6.5 dynamic_update_slice.24
  678.0 6.5 dynamic_update_slice.24
  690.4 6.5 dynamic_update_slice.24
  702.7 6.5 dynamic_update_slice.24
  715.1 6.5 dynamic_update_slice.24
  727.5 6.4 dynamic_update_slice.24
  739.8 6.5 dynamic_update_slice.24
  752.1 6.3 dynamic_update_slice.24
  764.3 6.3 dynamic_update_slice.24
  776.5 6.4 dynamic_update_slice.24
  788.7 6.4 dynamic_update_slice.24
  801.0 6.5 dynamic_update_slice.24
  813.4 6.0 dynamic_update_slice.24
  825.3 6.4 dynamic_update_slice.24
  837.5 6.5 dynamic_update_slice.24
  849.9 5.9 dynamic_update_slice.24
  861.7 6.2 dynamic_update_slice.24
  873.8 6.2 dynamic_update_slice.24
  885.8 6.4 dynamic_update_slice.24
  898.1 6.3 dynamic_update_slice.24
  910.3 6.5 dynamic_update_slice.24
  922.6 6.3 dynamic_update_slice.24
  934.8 6.1 dynamic_update_slice.24
  946.8 6.5 dynamic_update_slice.24
  959.1 6.0 dynamic_update_slice.24
  971.0 6.0 dynamic_update_slice.24
  982.9 6.5 dynamic_update_slice.24
  995.3 6.4 dynamic_update_slice.24
  (258 shorter events, 231.3 us)
Async XLA Ops:
  12.1 10.6 %all-to-all-start = ((s32[16,2,3]{2,1,0:T(2,128)}), s32[16,2,3]{2,1,0:T(2,128)S(1)}, u32[]{:S(2)}, u32[]{:S(2)}) async-start(s32[16,2,3]{2,1,0:T(2,128)} %copy.88), calls=%async_computation | async-start | bytes 32768 | tf_op jit(solution)/shard_map/all_to_all | solution.py:143
  22.8 89.2 %copy-start.6 = (s32[32,3]{0,1:T(4,128)}, s32[32,3]{0,1:T(4,128)S(1)}, u32[]{:S(2)}) copy-start(s32[32,3]{0,1:T(4,128)S(1)} %copy.109) | copy-start | bytes 1156
  112.0 0.9 copy-start
  112.9 137.8 %all-to-all-start.1 = ((bf16[16,2,2,256,256]{4,3,2,1,0:T(8,128)(2,1)}), bf16[16,2,2,256,256]{4,3,2,1,0:T(8,128)(2,1)}, u32[]{:S(2)}, u32[]{:S(2)}) async-start(bf16[16,2,2,256,256]{4,3,2,1,0:T(8,128)(2,1)} %bitcast.241), calls=%async_computation.1 | async-start | bytes 16777216 | tf_op jit(solution)/shard_map/all_to_all | solution.py:147
  250.7 6.2 copy-start.2
  268.2 1.6 copy-start.8
  298.3 1.6 copy-start.8
  317.1 7.5 copy-start.3
  331.8 9.4 copy-start.1
  331.8 279.5 %all-to-all-start.2 = ((bf16[16,2,2,256,256]{4,3,2,1,0:T(8,128)(2,1)}), bf16[16,2,2,256,256]{4,3,2,1,0:T(8,128)(2,1)}, u32[]{:S(2)}, u32[]{:S(2)}) async-start(bf16[16,2,2,256,256]{4,3,2,1,0:T(8,128)(2,1)} %broadcast_select_fusion), calls=%async_computation.2 | async-start | bytes 16777216 | tf_op jit(solution)/shard_map/all_to_all | solution.py:151
  341.2 268.2 %all-reduce.2.cloned.1.call-start = ((), (), s32[]{:S(2)}) async-start(), calls=%async_computation.3 | async-start | bytes 1048576 | tf_op jit(solution)/shard_map/psum | solution.py:162
  341.4 92.9 %collective-permute-start = (bf16[2,512,1]{2,1,0:T(8,128)(2,1)S(1)}, bf16[2,512,1]{2,1,0:T(8,128)(2,1)S(1)}, u32[]{:S(2)}, u32[]{:S(2)}) collective-permute-start(bf16[2,512,1]{2,1,0:T(8,128)(2,1)S(1)} %get-tuple-element.301), channel_id=1, source_target_pairs={{0,8},{8,16},{16,24},{24,32},{32,40},{40,48},{48,56},{56,64},{64,7... | collective-permute-start | bytes 6152 | tf_op jit(solution)/shard_map/ppermute | solution.py:14
  342.6 91.7 %collective-permute-start.1 = (bf16[2,512,1]{2,1,0:T(8,128)(2,1)S(1)}, bf16[2,512,1]{2,1,0:T(8,128)(2,1)S(1)}, u32[]{:S(2)}, u32[]{:S(2)}) collective-permute-start(bf16[2,512,1]{2,1,0:T(8,128)(2,1)S(1)} %get-tuple-element.302), channel_id=1, source_target_pairs={{8,0},{16,8},{24,16},{32,24},{40,32},{48,40},{56,48},{64,56},{72,6... | collective-permute-start | bytes 6152 | tf_op jit(solution)/shard_map/ppermute | solution.py:17
  434.3 0.7 copy-start.4
  435.0 0.7 copy-start.5
  435.7 12.1 %collective-permute-start.2 = (bf16[2,1,386]{2,1,0:T(2,128)(2,1)S(1)}, bf16[2,1,386]{2,1,0:T(2,128)(2,1)S(1)}, u32[]{:S(2)}, u32[]{:S(2)}) collective-permute-start(bf16[2,1,386]{2,1,0:T(2,128)(2,1)S(1)} %get-tuple-element.299), channel_id=1, source_target_pairs={{0,1},{1,2},{2,3},{3,4},{4,5},{5,6},{6,7},{7,0},{8,9},{9,10},{10,1... | collective-permute-start | bytes 4640 | tf_op jit(solution)/shard_map/ppermute | solution.py:14
  447.1 3.0 collective-permute-start.3
  454.1 157.2 %copy-start.7 = (s32[32,3]{0,1:T(4,128)S(1)}, s32[32,3]{0,1:T(4,128)}, u32[]{:S(2)}) copy-start(s32[32,3]{0,1:T(4,128)} %copy-done.6) | copy-start | bytes 1156
Sparse Core Ops, SparseCore 0:
  454.2 155.1 all-reduce.1
where the time goes:
time: 1020 us; the launch traced here: 1010 us
  waiting for transfers between devices  379 us (37%)
  local copies, waits for them, and re-layouts  335 us (33%)
  loops' own time  122 us (12%)
  other arithmetic  70.1 us (7%)
  matrix products  53 us (5%)
  starting transfers between devices  36.3 us (4%)
  between operations  14.1 us (1%)
    dynamic_update_slice x32, local copies, waits for them, and re-layouts, add_one(): lax.dynamic_update_slice(acc, window - 0.25 * grads[item].astype(jnp.floa...  203 us
    psum x1, waiting for transfers between devices, shards(): probe_grad = lax.psum(probe_part, ('pos', 'obj'))  151 us
    all_to_all x1, waiting for transfers between devices, shards(): lax.all_to_all(windows, 'pos', split_axis=0, concat_axis=0, tiled=True)  131 us
    another operation x1, loops' own time, add_scaled(): return lax.fori_loop(0, grads.shape[0], add_one, start_value)  121 us
    ppermute x2, waiting for transfers between devices, padded_2(): lax.ppermute(lax.slice_in_dim(block, block.shape[dim] - width, None, axis...  92.1 us
    gather x96, local copies, waits for them, and re-layouts  89.1 us
    sub x32, other arithmetic, add_one(): window - 0.25 * grads[item].astype(jnp.float32)  45.3 us
    dot_general x16, matrix products, product(): jnp.einsum('bjk,kl->bjl', values, matrix, preferred_element_type=jnp.floa...  28.6 us
  transfers between devices with their start and end apart: 8, of which 6 were waited for; matrix products, arithmetic and copies ran while one was open for 1% of the time, Pallas kernels for 0%

commit v1 on v0

--- a/solution.py
+++ b/solution.py
@@ -159,7 +159,9 @@
     corners = received.reshape(slots, 3)
     base = object_field - 0.125 * smooth
     new_object = add_scaled(base, incoming, corners, size)
-    probe_grad = lax.psum(probe_part, ("pos", "obj"))
+    probe_grad = probe_part
+    for idx in ("obj", "pos"):
+        probe_grad = lax.psum(probe_grad, axis_name=idx)
     n_total = pos_dev * n_pos * n_obj
     new_probe = probe - probe_grad * (1.0 / math.sqrt(n_total))
     return (new_object, new_probe)

time: 1020 us -> 987 us (0.968)
  waiting for transfers between devices: 379 us -> 295 us
  local copies, waits for them, and re-layouts: 335 us -> 394 us
  other arithmetic: 70.1 us -> 58.7 us
    ppermute x2, waiting for transfers between devices: 92.1 us -> 23.9 us  [padded_2(): lax.ppermute(lax.slice_in_dim(block, block.shape[dim] - width, None, axis...]
    dynamic_update_slice x32, local copies, waits for them, and re-layouts: 203 us -> 263 us  [add_one(): lax.dynamic_update_slice(acc, window - 0.25 * grads[item].astype(jnp.floa...]
    psum x1 -> x2, waiting for transfers between devices: 151 us -> 136 us  [shards(): probe_grad = lax.psum(probe_grad, axis_name=idx)]
  transfers between devices with their start and end apart: 8 -> 9, of which waited for: 6 -> 7; matrix products, arithmetic and copies ran while one was open for 1% -> 1% of each run, Pallas kernels for 0% -> 0%
where the time goes in v1:
time: 987 us; the launch traced here: 977 us
  local copies, waits for them, and re-layouts  394 us (40%)
  waiting for transfers between devices  295 us (30%)
  loops' own time  126 us (13%)
  other arithmetic  58.7 us (6%)
  matrix products  53 us (5%)
  starting transfers between devices  36.2 us (4%)
  between operations  14.2 us (1%)
    dynamic_update_slice x32, local copies, waits for them, and re-layouts, add_one(): lax.dynamic_update_slice(acc, window - 0.25 * grads[item].astype(jnp.floa...  263 us
    psum x2, waiting for transfers between devices, shards(): probe_grad = lax.psum(probe_grad, axis_name=idx)  136 us
    all_to_all x1, waiting for transfers between devices, shards(): lax.all_to_all(windows, 'pos', split_axis=0, concat_axis=0, tiled=True)  131 us
    another operation x1, loops' own time, add_scaled(): return lax.fori_loop(0, grads.shape[0], add_one, start_value)  126 us
    gather x96, local copies, waits for them, and re-layouts  88.2 us
    sub x32, other arithmetic, add_one(): window - 0.25 * grads[item].astype(jnp.float32)  37.3 us
    dot_general x16, matrix products, product(): jnp.einsum('bjk,kl->bjl', values, matrix, preferred_element_type=jnp.floa...  28.6 us
    dot_general x16, matrix products, product(): jnp.einsum('jk,bkl->bjl', matrix, values, preferred_element_type=jnp.floa...  24.5 us
  transfers between devices with their start and end apart: 9, of which 7 were waited for; matrix products, arithmetic and copies ran while one was open for 1% of the time, Pallas kernels for 0%

profile of v1, /device:TPU:15, one launch (start us, length us, event | category | flops | bytes accessed | tf_op | source)
XLA Modules:
  0.0 977.3 jit_solution(16186949601398293141)
XLA Ops:
  12.1 6.8 all-to-all-start
  22.9 88.3 %while.29 = (s32[]{:T(128)}, bf16[2,512,384]{2,1,0:T(8,128)(2,1)S(1)}, s32[32,3]{0,1:T(4,128)S(1)}, bf16[32,2,256,256]{3,2,1,0:T(8,128)(2,1)}, s32[]{:T(128)}) while((s32[]{:T(128)}, bf16[2,512,384]{2,1,0:T(8,128)(2,1)S(1)}, s32[32,3]{0,1:T(4,128)S(1)}, bf16[32,2,256,256]{3,2,1,0:T(8,128)(2,1)}, s32[]{:T(128)}) %tuple.89), condition=%wide.while_cond, body=%wide.while_body.sunk | while | flops 2 | bytes 525929 | solution.py:101
  112.0 7.2 all-to-all-start.1
  119.3 130.6 %all-to-all-done.1 = bf16[16,2,2,256,256]{4,3,2,1,0:T(8,128)(2,1)} async-done(((bf16[16,2,2,256,256]{4,3,2,1,0:T(8,128)(2,1)}), bf16[16,2,2,256,256]{4,3,2,1,0:T(8,128)(2,1)}, u32[]{:S(2)}, u32[]{:S(2)}) %all-to-all-start.1) | async-done | bytes 8388640 | tf_op jit(solution)/shard_map/all_to_all | solution.py:147
  249.9 6.2 gather_fusion.1
  256.1 60.2 %while.30 = (s32[]{:T(128)}, bf16[2,8,2,256,256]{4,3,2,1,0:T(8,128)(2,1)}, f32[2,2,256,256]{3,2,1,0:T(8,128)S(1)}, f32[2,256,256]{2,1,0:T(8,128)S(1)}, bf16[2,8,...) while((s32[]{:T(128)}, ...), condition=%wide.region_7.8_spmd.clone.clone, body=%wide.region_4.7_spmd.clone.clone.sunk | while | flops 4348182528 | bytes 96470128 | solution.py:93
  281.6 3.0 fusion.253
  311.7 3.0 fusion.253
  316.3 7.1 gather_fusion.2
  323.4 7.2 broadcast_select_fusion
  330.6 9.3 all-to-all-start.2
  342.8 67.9 %all-reduce.3.cloned.1.call-done = f32[2,256,256]{2,1,0:T(8,128)} async-done(((f32[2,256,256]{2,1,0:T(8,128)}), f32[2,256,256]{2,1,0:T(8,128)}) %all-reduce.3.cloned.1.call-update) | async-done | bytes 524304 | tf_op jit(solution)/shard_map/psum | solution.py:164
  410.7 23.2 %collective-permute-done = bf16[2,512,1]{2,1,0:T(8,128)(2,1)S(1)} collective-permute-done((bf16[2,512,1]{2,1,0:T(8,128)(2,1)S(1)}, bf16[2,512,1]{2,1,0:T(8,128)(2,1)S(1)}, u32[]{:S(2)}, u32[]{:S(2)}) %collective-permute-start) | collective-permute-done | bytes 2080 | tf_op jit(solution)/shard_map/ppermute | solution.py:14
  434.0 11.3 %collective-permute-start.2 = (bf16[2,1,386]{2,1,0:T(2,128)(2,1)S(1)}, bf16[2,1,386]{2,1,0:T(2,128)(2,1)S(1)}, u32[]{:S(2)}, u32[]{:S(2)}) collective-permute-start(bf16[2,1,386]{2,1,0:T(2,128)(2,1)S(1)} %get-tuple-element.299), channel_id=1, source_target_pairs={{0,1},{1,2},{2,3},{3,4},{4,5},{5,6},{6,7},{7,0},{8,9},{9,10},{10,1... | collective-permute-start | bytes 4640 | tf_op jit(solution)/shard_map/ppermute | solution.py:14
  452.0 68.2 %all-reduce.5.cloned.1.call-done = f32[2,256,256]{2,1,0:T(8,128)} async-done(((f32[2,256,256]{2,1,0:T(8,128)}), f32[2,256,256]{2,1,0:T(8,128)}) %all-reduce.5.cloned.1.call-update) | async-done | bytes 524304 | tf_op jit(solution)/shard_map/psum | solution.py:164
  522.1 447.2 %while.28 = (s32[]{:T(128)}, f32[2,512,384]{2,1,0:T(8,128)S(1)}, s32[32,3]{0,1:T(4,128)S(1)}, bf16[32,2,256,256]{3,2,1,0:T(8,128)(2,1)}, s32[]{:T(128)}, /*index=5*/s32[]{:T(128)}, s32[]{:T(128)}, s32[]{:T(128)}) while((s32[]{:T(128)}, f32[2,512,384]{2,1,0:T(8,128)S(1)}, s32[32,3]{0,1:T(4,128)S(1)}, bf16[32,2,256,256]{3,2,1,0:T(8,128)(2,1)}, ...), condition=%wide.region_9.10_spmd, body=%wide.region_8.9_spmd.sunk | while | flops 393224 | bytes 2359485 | solution.py:117
  527.8 8.3 dynamic_update_slice.24
  541.9 7.4 dynamic_update_slice.24
  555.0 8.7 dynamic_update_slice.24
  569.5 7.3 dynamic_update_slice.24
  582.5 9.2 dynamic_update_slice.24
  597.4 8.8 dynamic_update_slice.24
  612.0 8.9 dynamic_update_slice.24
  626.6 9.2 dynamic_update_slice.24
  641.6 9.2 dynamic_update_slice.24
  656.6 8.4 dynamic_update_slice.24
  670.8 8.8 dynamic_update_slice.24
  685.4 8.0 dynamic_update_slice.24
  699.2 7.8 dynamic_update_slice.24
  712.7 8.1 dynamic_update_slice.24
  726.6 8.4 dynamic_update_slice.24
  740.8 9.2 dynamic_update_slice.24
  755.7 7.3 dynamic_update_slice.24
  768.7 8.1 dynamic_update_slice.24
  782.5 9.2 dynamic_update_slice.24
  797.5 7.0 dynamic_update_slice.24
  810.3 7.7 dynamic_update_slice.24
  823.7 7.5 dynamic_update_slice.24
  837.0 8.2 dynamic_update_slice.24
  850.9 7.9 dynamic_update_slice.24
  864.6 8.6 dynamic_update_slice.24
  878.9 8.0 dynamic_update_slice.24
  892.6 7.4 dynamic_update_slice.24
  905.8 8.8 dynamic_update_slice.24
  920.4 7.3 dynamic_update_slice.24
  933.4 7.3 dynamic_update_slice.24
  946.4 8.9 dynamic_update_slice.24
  961.1 8.2 dynamic_update_slice.24
  (257 shorter events, 222.9 us)
Async XLA Ops:
  12.1 10.6 %all-to-all-start = ((s32[16,2,3]{2,1,0:T(2,128)}), s32[16,2,3]{2,1,0:T(2,128)S(1)}, u32[]{:S(2)}, u32[]{:S(2)}) async-start(s32[16,2,3]{2,1,0:T(2,128)} %copy.88), calls=%async_computation | async-start | bytes 32768 | tf_op jit(solution)/shard_map/all_to_all | solution.py:143
  22.8 88.4 %copy-start.4 = (s32[32,3]{0,1:T(4,128)}, s32[32,3]{0,1:T(4,128)S(1)}, u32[]{:S(2)}) copy-start(s32[32,3]{0,1:T(4,128)S(1)} %copy.109) | copy-start | bytes 1156
  111.2 0.9 copy-start
  112.0 137.8 %all-to-all-start.1 = ((bf16[16,2,2,256,256]{4,3,2,1,0:T(8,128)(2,1)}), bf16[16,2,2,256,256]{4,3,2,1,0:T(8,128)(2,1)}, u32[]{:S(2)}, u32[]{:S(2)}) async-start(bf16[16,2,2,256,256]{4,3,2,1,0:T(8,128)(2,1)} %bitcast.241), calls=%async_computation.1 | async-start | bytes 16777216 | tf_op jit(solution)/shard_map/all_to_all | solution.py:147
  249.9 6.2 copy-start.2
  267.4 1.6 copy-start.6
  297.5 1.6 copy-start.6
  330.6 191.5 %all-to-all-start.2 = ((bf16[16,2,2,256,256]{4,3,2,1,0:T(8,128)(2,1)}), bf16[16,2,2,256,256]{4,3,2,1,0:T(8,128)(2,1)}, u32[]{:S(2)}, u32[]{:S(2)}) async-start(bf16[16,2,2,256,256]{4,3,2,1,0:T(8,128)(2,1)} %broadcast_select_fusion), calls=%async_computation.2 | async-start | bytes 16777216 | tf_op jit(solution)/shard_map/all_to_all | solution.py:151
  339.9 1.3 copy-start.1
  339.9 70.8 %all-reduce.3.cloned.1.call-start = ((), (), s32[]{:S(2)}) async-start(), calls=%async_computation.3 | async-start | bytes 1048576 | tf_op jit(solution)/shard_map/psum | solution.py:164
  340.8 179.4 %all-reduce.5.cloned.1.call-start = ((), (), s32[]{:S(2)}) async-start(), calls=%async_computation.4 | async-start | bytes 1048576 | tf_op jit(solution)/shard_map/psum | solution.py:164
  341.3 92.6 %collective-permute-start = (bf16[2,512,1]{2,1,0:T(8,128)(2,1)S(1)}, bf16[2,512,1]{2,1,0:T(8,128)(2,1)S(1)}, u32[]{:S(2)}, u32[]{:S(2)}) collective-permute-start(bf16[2,512,1]{2,1,0:T(8,128)(2,1)S(1)} %get-tuple-element.301), channel_id=1, source_target_pairs={{0,8},{8,16},{16,24},{24,32},{32,40},{40,48},{48,56},{56,64},{64,7... | collective-permute-start | bytes 6152 | tf_op jit(solution)/shard_map/ppermute | solution.py:14
  342.5 91.4 %collective-permute-start.1 = (bf16[2,512,1]{2,1,0:T(8,128)(2,1)S(1)}, bf16[2,512,1]{2,1,0:T(8,128)(2,1)S(1)}, u32[]{:S(2)}, u32[]{:S(2)}) collective-permute-start(bf16[2,512,1]{2,1,0:T(8,128)(2,1)S(1)} %get-tuple-element.302), channel_id=1, source_target_pairs={{8,0},{16,8},{24,16},{32,24},{40,32},{48,40},{56,48},{64,56},{72,6... | collective-permute-start | bytes 6152 | tf_op jit(solution)/shard_map/ppermute | solution.py:17
  434.0 12.1 %collective-permute-start.2 = (bf16[2,1,386]{2,1,0:T(2,128)(2,1)S(1)}, bf16[2,1,386]{2,1,0:T(2,128)(2,1)S(1)}, u32[]{:S(2)}, u32[]{:S(2)}) collective-permute-start(bf16[2,1,386]{2,1,0:T(2,128)(2,1)S(1)} %get-tuple-element.299), channel_id=1, source_target_pairs={{0,1},{1,2},{2,3},{3,4},{4,5},{5,6},{6,7},{7,0},{8,9},{9,10},{10,1... | collective-permute-start | bytes 4640 | tf_op jit(solution)/shard_map/ppermute | solution.py:14
  445.3 3.0 collective-permute-start.3
  449.2 72.9 %copy-start.5 = (s32[32,3]{0,1:T(4,128)S(1)}, s32[32,3]{0,1:T(4,128)}, u32[]{:S(2)}) copy-start(s32[32,3]{0,1:T(4,128)} %copy-done.4) | copy-start | bytes 1156
  969.3 1.1 copy-start.3
Sparse Core Ops, SparseCore 0:
  343.6 67.0 all-reduce.2
  414.2 105.9 all-reduce.4
